TPU v7x, 32 devices: a whole 2x2x4 slice. The times are simulated.
32 devices in a mesh: section: 2 (over core), dp: 8 (over z, x), tensor: 2 (over y).
Axes of the slice: x: 2, y: 2, z: 4, core: 2. Of those that a mesh axis runs over, the one named last changes fastest.
Arguments:
- inputs: float32 [2048, 1024], P(('dp', 'tensor')), may hold values from -6 to 6
- segments: int32 [2048], P('dp'), may hold values from 0 to 1, never falling along the last dimension, each value on 1 to 1536 neighbouring positions
- mixer_gain: float32 [2, 1024], P('section', ('dp', 'tensor')), may hold values from 0.25 to 1.75
- query_weight: bfloat16 [2, 1024, 512], P('section', 'dp', 'tensor'), may hold values from -0.1875 to 0.1875
- key_weight: bfloat16 [2, 1024, 512], P('section', 'dp', 'tensor'), may hold values from -0.1875 to 0.1875
- value_weight: bfloat16 [2, 1024, 1024], P('section', 'dp', 'tensor'), may hold values from -0.1875 to 0.1875
- outgate_weight: bfloat16 [2, 1024, 1024], P('section', 'dp', 'tensor'), may hold values from -0.1875 to 0.1875
- decay_down: float32 [2, 1024, 16], P('section', ('dp', 'tensor')), may hold values from -0.1875 to 0.1875
- decay_up: float32 [2, 16, 512], P('section', None, ('dp', 'tensor')), may hold values from -1.5 to 1.5
- decay_bias: float32 [2, 512], P('section', ('dp', 'tensor')), may hold values from -3 to 7
- head_gain: float32 [2, 256], P('section', ('dp', 'tensor')), may hold values from 0.25 to 1.75
- output_weight: bfloat16 [2, 1024, 1024], P('section', 'tensor', 'dp'), may hold values from -0.1875 to 0.1875
- feed_gain: float32 [2, 1024], P('section', ('dp', 'tensor')), may hold values from 0.25 to 1.75
- gate_weight: bfloat16 [2, 1024, 2816], P('section', 'dp', 'tensor'), may hold values from -0.1875 to 0.1875
- up_weight: bfloat16 [2, 1024, 2816], P('section', 'dp', 'tensor'), may hold values from -0.1875 to 0.1875
- down_weight: bfloat16 [2, 2816, 1024], P('section', 'tensor', 'dp'), may hold values from -0.109375 to 0.109375
- cotangent: float32 [2048, 1024], P(('dp', 'tensor')), may hold values from -6 to 6
Outputs:
- section_outputs: float32 [2, 2048, 1024], P('section', ('dp', 'tensor'))
- input_grads: float32 [2, 2048, 1024], P('section', ('dp', 'tensor'))
- mixer_grad: float32 [2, 1024], P('section', ('dp', 'tensor'))
- query_grad: float32 [2, 1024, 512], P('section', 'dp', 'tensor')
- key_grad: float32 [2, 1024, 512], P('section', 'dp', 'tensor')
- value_grad: float32 [2, 1024, 1024], P('section', 'dp', 'tensor')
- outgate_grad: float32 [2, 1024, 1024], P('section', 'dp', 'tensor')
- downrank_grad: float32 [2, 1024, 16], P('section', ('dp', 'tensor'))
- uprank_grad: float32 [2, 16, 512], P('section', None, ('dp', 'tensor'))
- bias_grad: float32 [2, 512], P('section', ('dp', 'tensor'))
- headgain_grad: float32 [2, 256], P('section', ('dp', 'tensor'))
- output_grad: float32 [2, 1024, 1024], P('section', 'tensor', 'dp')
- feed_grad: float32 [2, 1024], P('section', ('dp', 'tensor'))
- gate_grad: float32 [2, 1024, 2816], P('section', 'dp', 'tensor')
- up_grad: float32 [2, 1024, 2816], P('section', 'dp', 'tensor')
- down_grad: float32 [2, 2816, 1024], P('section', 'tensor', 'dp')
Inputs may be any that keep to these rules, and one draw needn't show every extreme that they name: `segments`: segment numbers never fall along the tokens; each of the 2 documents covers 1 to 1536 consecutive tokens,.
All inputs are finite; a program needn't handle non-finite values.
Results may differ from a plain program's by a relative error of at most 0.03.
Values may be sent and summed in bfloat16 or wider, within the bound.
No kernel may reach another device: no remote copies, remote signals or barrier semaphores. Data moves between devices by JAX's collectives and lax.ppermute only.
A program may use at most 128 MiB of HBM per device.

v0:
```python
import jax
import jax.numpy as jnp
from jax import lax
from jax.sharding import PartitionSpec as P

HEADS = 4
KDIM = 128
VDIM = 256
RANK = 16
GROUP = 64


exact_mode = lax.Precision.HIGHEST
norm_eps = 1e-06
head_eps = 1e-05


def carried_in(shard, axis, combine, identity):
    length, here = (lax.axis_size(axis), lax.axis_index(axis))
    everything = jax.tree.map(
        lambda part, kind: lax.all_gather(part.astype(kind), axis),
        shard,
        (jnp.bfloat16, jnp.bfloat16, jnp.bfloat16, jnp.bfloat16),
    )
    start = jax.tree.map(
        lambda part, zero: jnp.broadcast_to(jnp.asarray(zero, part.dtype), part.shape),
        shard,
        identity,
    )

    def lap(k, before):
        reached = k < here
        new = combine(
            before, jax.tree.map(lambda part, own: part[k].astype(own.dtype), everything, shard)
        )
        return jax.tree.map(lambda a, b: jnp.where(reached, a, b), new, before)

    return lax.fori_loop(0, length, lap, start)


def carried_in_2(shard, axis, combine, identity):
    length, here = (lax.axis_size(axis), lax.axis_index(axis))
    everything = jax.tree.map(
        lambda part, kind: lax.all_gather(part.astype(kind), axis),
        shard,
        jax.tree.map(lambda a: jnp.bfloat16 if a.dtype == jnp.float32 else a.dtype, shard),
    )
    start = jax.tree.map(
        lambda part, zero: jnp.broadcast_to(jnp.asarray(zero, part.dtype), part.shape),
        shard,
        identity,
    )

    def lap(k, before):
        at = length - 1 - k
        reached = at > here
        new = combine(
            before, jax.tree.map(lambda part, own: part[at].astype(own.dtype), everything, shard)
        )
        return jax.tree.map(lambda a, b: jnp.where(reached, a, b), new, before)

    return lax.fori_loop(0, length, lap, start)


def shifted(block, axis, distance):
    devices = range(lax.axis_size(axis))
    route = [(i - distance, i) for i in devices if i - distance in devices]
    return lax.ppermute(block, axis, route)


def product(left, right):
    return jnp.dot(left, right, preferred_element_type=jnp.float32)


def exact_product(left, right):
    return jnp.dot(left, right, precision=exact_mode, preferred_element_type=jnp.float32)


def rms_scale(values, epsilon):
    return lax.rsqrt(jnp.mean(values * values, axis=-1, keepdims=True) + epsilon)


def to_heads(values, column_count):
    token_count = values.shape[0]
    return values.reshape(token_count, -1, column_count).transpose(1, 0, 2)


def from_heads(values):
    head_count, token_count, column_count = values.shape
    return values.transpose(1, 0, 2).reshape(token_count, head_count * column_count)


def norm_back(grad_unit, unit_values, scale_values):
    return scale_values * (
        grad_unit - unit_values * jnp.mean(grad_unit * unit_values, axis=-1, keepdims=True)
    )


def silu_slope(values):
    sigma = jax.nn.sigmoid(values)
    return sigma * (1.0 + values * (1.0 - sigma))


def gla_groups(
    query_heads, key_heads, value_heads, decay_heads, segment_ids, state_start, segment_before
):
    head_count, token_count, key_width = query_heads.shape
    value_width = value_heads.shape[2]
    block_count = token_count // GROUP

    def to_blocks(tensor):
        return tensor.reshape(head_count, block_count, GROUP, tensor.shape[2]).transpose(1, 0, 2, 3)

    positions = jnp.arange(GROUP)
    causal = positions[:, None] >= positions[None, :]

    def advance(running, pieces):
        state_now, segment_prev = running
        query_block, key_block, value_block, decay_block, segment_block = pieces
        decay_sums = jnp.cumsum(decay_block, axis=1)
        allowed = causal & (segment_block[:, None] == segment_block[None, :])
        allowed_full = allowed[None, :, :, None]
        spans = decay_sums[:, :, None, :] - decay_sums[:, None, :, :]
        factors = jnp.where(allowed_full, jnp.exp(jnp.where(allowed_full, spans, 0.0)), 0.0)
        scores = jnp.sum(query_block[:, :, None, :] * key_block[:, None, :, :] * factors, axis=-1)
        within = jnp.einsum("hts,hse->hte", scores, value_block, precision=exact_mode)
        carried = jnp.where(
            (segment_block == segment_prev)[None, :, None], query_block * jnp.exp(decay_sums), 0.0
        )
        across = jnp.einsum("htd,hde->hte", carried, state_now, precision=exact_mode)
        block_end = decay_sums[:, GROUP - 1 :, :]
        segment_end = segment_block[GROUP - 1]
        kept_keys = jnp.where(
            (segment_block == segment_end)[None, :, None],
            key_block * jnp.exp(block_end - decay_sums),
            0.0,
        )
        factor = jnp.where(segment_end == segment_prev, jnp.exp(block_end[:, 0, :]), 0.0)
        state_next = factor[:, :, None] * state_now + jnp.einsum(
            "hsd,hse->hde", kept_keys, value_block, precision=exact_mode
        )
        return ((state_next, segment_end), within + across)

    pieces = (
        to_blocks(query_heads),
        to_blocks(key_heads),
        to_blocks(value_heads),
        to_blocks(decay_heads),
        segment_ids.reshape(block_count, GROUP),
    )
    (state_end, _), outputs = lax.scan(
        jax.checkpoint(advance), (state_start, segment_before), pieces
    )
    return (outputs.transpose(1, 0, 2, 3).reshape(head_count, token_count, value_width), state_end)


def join_forward(earlier, later):
    decay_low, state_low, first_low, last_low = earlier
    decay_high, state_high, first_high, last_high = later
    linked = jnp.where((first_high == last_low) | (last_low < 0.0) | (first_high < 0.0), 1.0, 0.0)
    decay_joined = decay_low * decay_high * linked
    state_joined = state_high + (decay_high * linked)[:, :, None] * state_low
    first_joined = jnp.where(first_low < 0.0, first_high, first_low)
    last_joined = jnp.where(last_high < 0.0, last_low, last_high)
    return (decay_joined, state_joined, first_joined, last_joined)


def join_backward(earlier, later):
    decay_high, grad_high, first_high, last_high = earlier
    decay_low, grad_low, first_low, last_low = later
    linked = jnp.where((first_high == last_low) | (last_low < 0.0) | (first_high < 0.0), 1.0, 0.0)
    decay_joined = decay_low * decay_high * linked
    grad_joined = grad_low + (decay_low * linked)[:, :, None] * grad_high
    first_joined = jnp.where(first_low < 0.0, first_high, first_low)
    last_joined = jnp.where(last_high < 0.0, last_low, last_high)
    return (decay_joined, grad_joined, first_joined, last_joined)


def gather_rows(values):
    return lax.all_gather(values, "tensor", axis=0, tiled=True)


def scatter_rows(values):
    return lax.psum_scatter(values, "tensor", scatter_dimension=0, tiled=True)


def gather_cotan(values):
    return lax.all_gather(values, "tensor", axis=0, tiled=True)


def scatter_cotan(values):
    return lax.psum_scatter(
        values.astype(jnp.bfloat16), "tensor", scatter_dimension=0, tiled=True
    ).astype(jnp.float32)


def layer_forward(layer_in, segment_ids, params):
    (
        query_weight,
        key_weight,
        value_weight,
        outgate_weight,
        output_weight,
        gate_weight,
        up_weight,
        down_weight,
        mixer_gain,
        feed_gain,
        decay_down,
        decay_up,
        decay_bias,
        head_gain,
    ) = params
    scale_one = rms_scale(layer_in, norm_eps)
    normed_one = (layer_in * scale_one * mixer_gain).astype(jnp.bfloat16)
    hidden_one = gather_rows(normed_one)
    query_heads = to_heads(product(hidden_one, query_weight), KDIM)
    key_heads = to_heads(product(hidden_one, key_weight), KDIM)
    value_heads = to_heads(product(hidden_one, value_weight), VDIM)
    outgate_heads = to_heads(product(hidden_one, outgate_weight), VDIM)
    latent = exact_product(hidden_one.astype(jnp.float32), decay_down)
    logits = exact_product(latent, decay_up) + decay_bias
    decay_heads = to_heads(jax.nn.log_sigmoid(logits) / 16.0, KDIM)
    decay_sums = jnp.cumsum(decay_heads, axis=1)
    decay_total = decay_sums[:, -1:, :]
    tail_keys = jnp.where(
        (segment_ids == segment_ids[-1])[None, :, None],
        key_heads * jnp.exp(decay_total - decay_sums),
        0.0,
    )
    summary = jnp.einsum("hsd,hse->hde", tail_keys, value_heads, precision=exact_mode)
    through = jnp.where(segment_ids[-1] == segment_ids[0], jnp.exp(decay_total[:, 0, :]), 0.0)
    bounds = -jnp.ones_like(segment_ids[:1])
    identity = (jnp.ones_like(through), jnp.zeros_like(summary), bounds, bounds)
    _, state_in, _, before = carried_in(
        (through, summary, segment_ids[:1], segment_ids[-1:]), "dp", join_forward, identity
    )
    mixed_heads, _ = gla_groups(
        query_heads, key_heads, value_heads, decay_heads, segment_ids, state_in, before[0]
    )
    scale_head = rms_scale(mixed_heads, head_eps)
    unit_head = mixed_heads * scale_head
    branch = from_heads(unit_head * head_gain * jax.nn.silu(outgate_heads)).astype(jnp.bfloat16)
    mid_stream = layer_in + scatter_rows(product(branch, output_weight))
    scale_two = rms_scale(mid_stream, norm_eps)
    normed_two = (mid_stream * scale_two * feed_gain).astype(jnp.bfloat16)
    hidden_two = gather_rows(normed_two)
    gate_pre = product(hidden_two, gate_weight)
    up_pre = product(hidden_two, up_weight)
    inner_act = (jax.nn.silu(gate_pre) * up_pre).astype(jnp.bfloat16)
    result = mid_stream + scatter_rows(product(inner_act, down_weight))
    saved = (
        layer_in,
        scale_one,
        hidden_one,
        query_heads,
        key_heads,
        value_heads,
        decay_heads,
        outgate_heads,
        latent,
        logits,
        decay_sums,
        through,
        state_in,
        before,
        scale_head,
        unit_head,
        branch,
        mid_stream,
        scale_two,
        hidden_two,
        gate_pre,
        up_pre,
        inner_act,
    )
    return (result, saved)


def layer_backward(saved, cotangent_in, segment_ids, params):
    (
        query_weight,
        key_weight,
        value_weight,
        outgate_weight,
        output_weight,
        gate_weight,
        up_weight,
        down_weight,
        mixer_gain,
        feed_gain,
        decay_down,
        decay_up,
        decay_bias,
        head_gain,
    ) = params
    (
        layer_in,
        scale_one,
        hidden_one,
        query_heads,
        key_heads,
        value_heads,
        decay_heads,
        outgate_heads,
        latent,
        logits,
        decay_sums,
        through,
        state_in,
        before,
        scale_head,
        unit_head,
        branch,
        mid_stream,
        scale_two,
        hidden_two,
        gate_pre,
        up_pre,
        inner_act,
    ) = saved
    cot_full = gather_cotan(cotangent_in.astype(jnp.bfloat16))
    inner_delta = product(cot_full, down_weight.T)
    down_grad = product(inner_act.T, cot_full)
    gate_delta = (inner_delta * up_pre * silu_slope(gate_pre)).astype(jnp.bfloat16)
    up_delta = (inner_delta * jax.nn.silu(gate_pre)).astype(jnp.bfloat16)
    hidden_two_delta = product(gate_delta, gate_weight.T) + product(up_delta, up_weight.T)
    gate_grad = product(hidden_two.T, gate_delta)
    up_grad = product(hidden_two.T, up_delta)
    normed_two_delta = scatter_cotan(hidden_two_delta)
    unit_two = mid_stream * scale_two
    feed_grad = jnp.sum(normed_two_delta * unit_two, axis=0)
    mid_delta = cotangent_in + norm_back(normed_two_delta * feed_gain, unit_two, scale_two)
    mid_full = gather_cotan(mid_delta.astype(jnp.bfloat16))
    branch_delta = to_heads(product(mid_full, output_weight.T), VDIM)
    output_grad = product(branch.T, mid_full)
    swish = jax.nn.silu(outgate_heads)
    unit_delta = branch_delta * swish * head_gain
    outgate_delta = branch_delta * unit_head * head_gain * silu_slope(outgate_heads)
    headgain_grad = jnp.sum(branch_delta * swish * unit_head, axis=(0, 1))
    mixed_delta = norm_back(unit_delta, unit_head, scale_head)
    opened = jnp.where(
        (segment_ids == segment_ids[0])[None, :, None], query_heads * jnp.exp(decay_sums), 0.0
    )
    local_term = jnp.einsum("htd,hte->hde", opened, mixed_delta, precision=exact_mode)
    bounds = -jnp.ones_like(segment_ids[:1])
    identity = (jnp.ones_like(through), jnp.zeros_like(local_term), bounds, bounds)
    _, from_later, later_first, _ = carried_in_2(
        (through, local_term, segment_ids[:1], segment_ids[-1:]), "dp", join_backward, identity
    )
    end_grad = jnp.where(later_first[0] == segment_ids[-1], from_later, 0.0)

    def recurrence(query_part, key_part, value_part, decay_part):
        return gla_groups(
            query_part, key_part, value_part, decay_part, segment_ids, state_in, before[0]
        )

    _, pull_back = jax.vjp(recurrence, query_heads, key_heads, value_heads, decay_heads)
    query_delta, key_delta, value_delta, decay_delta = pull_back((mixed_delta, end_grad))
    logit_delta = from_heads(decay_delta) * jax.nn.sigmoid(-logits) / 16.0
    bias_grad = jnp.sum(logit_delta, axis=0)
    uprank_grad = exact_product(latent.T, logit_delta)
    latent_delta = exact_product(logit_delta, decay_up.T)
    query_low = from_heads(query_delta).astype(jnp.bfloat16)
    key_low = from_heads(key_delta).astype(jnp.bfloat16)
    value_low = from_heads(value_delta).astype(jnp.bfloat16)
    outgate_low = from_heads(outgate_delta).astype(jnp.bfloat16)
    hidden_one_delta = (
        product(query_low, query_weight.T)
        + product(key_low, key_weight.T)
        + product(value_low, value_weight.T)
        + product(outgate_low, outgate_weight.T)
        + exact_product(latent_delta, decay_down.T)
    )
    query_grad = product(hidden_one.T, query_low)
    key_grad = product(hidden_one.T, key_low)
    value_grad = product(hidden_one.T, value_low)
    outgate_grad = product(hidden_one.T, outgate_low)
    downrank_grad = exact_product(hidden_one.astype(jnp.float32).T, latent_delta)
    normed_one_delta = scatter_cotan(hidden_one_delta)
    unit_one = layer_in * scale_one
    mixer_grad = jnp.sum(normed_one_delta * unit_one, axis=0)
    input_delta = mid_delta + norm_back(normed_one_delta * mixer_gain, unit_one, scale_one)
    big_grads = (
        query_grad,
        key_grad,
        value_grad,
        outgate_grad,
        output_grad,
        gate_grad,
        up_grad,
        down_grad,
    )
    small_grads = (mixer_grad, feed_grad, downrank_grad, uprank_grad, bias_grad, headgain_grad)
    return (input_delta, big_grads, small_grads)


def lifted(array):
    return array[None]


def shards(
    inputs,
    segments,
    mixer_gain,
    query_weight,
    key_weight,
    value_weight,
    outgate_weight,
    decay_down,
    decay_up,
    decay_bias,
    head_gain,
    output_weight,
    feed_gain,
    gate_weight,
    up_weight,
    down_weight,
    cotangent,
):
    section_index = lax.axis_index("section")
    tensor_index = lax.axis_index("tensor")
    on_first = section_index == 0
    big_weights = (
        lax.all_gather(query_weight[0], "dp", axis=0, tiled=True),
        lax.all_gather(key_weight[0], "dp", axis=0, tiled=True),
        lax.all_gather(value_weight[0], "dp", axis=0, tiled=True),
        lax.all_gather(outgate_weight[0], "dp", axis=0, tiled=True),
        lax.all_gather(output_weight[0], "dp", axis=1, tiled=True),
        lax.all_gather(gate_weight[0], "dp", axis=0, tiled=True),
        lax.all_gather(up_weight[0], "dp", axis=0, tiled=True),
        lax.all_gather(down_weight[0], "dp", axis=1, tiled=True),
    )
    small_params = (
        lax.all_gather(mixer_gain[0], ("dp", "tensor"), axis=0, tiled=True),
        lax.all_gather(feed_gain[0], ("dp", "tensor"), axis=0, tiled=True),
        lax.all_gather(decay_down[0], ("dp", "tensor"), axis=0, tiled=True),
        lax.all_gather(decay_up[0], ("dp", "tensor"), axis=1, tiled=True),
        lax.all_gather(decay_bias[0], ("dp", "tensor"), axis=0, tiled=True),
        lax.all_gather(head_gain[0], ("dp", "tensor"), axis=0, tiled=True),
    )
    column_width = HEADS // lax.axis_size("tensor") * KDIM
    column_start = tensor_index * column_width
    up_local = lax.dynamic_slice_in_dim(small_params[3], column_start, column_width, 1)
    bias_local = lax.dynamic_slice_in_dim(small_params[4], column_start, column_width, 0)
    params = tuple(big_weights) + (
        small_params[0],
        small_params[1],
        small_params[2],
        up_local,
        bias_local,
        small_params[5],
    )
    segment_ids = segments.astype(jnp.float32)
    first_out, first_saved = layer_forward(inputs, segment_ids, params)
    received = shifted(first_out, "section", 1)
    second_out, second_saved = layer_forward(received, segment_ids, params)
    section_out = jnp.where(on_first, first_out, second_out)
    late_delta, late_big, late_small = layer_backward(second_saved, cotangent, segment_ids, params)
    returned = shifted(late_delta.astype(jnp.bfloat16), "section", -1).astype(late_delta.dtype)
    early_delta, early_big, early_small = layer_backward(first_saved, returned, segment_ids, params)
    input_grad = jnp.where(on_first, early_delta, late_delta)

    def pick(first_part, second_part):
        return jnp.where(on_first, first_part, second_part)

    chosen_small = jax.tree.map(pick, early_small, late_small)
    uprank_full = lax.dynamic_update_slice_in_dim(
        jnp.zeros((RANK, HEADS * KDIM), jnp.float32), chosen_small[3], column_start, 1
    )
    bias_full = lax.dynamic_update_slice_in_dim(
        jnp.zeros((HEADS * KDIM,), jnp.float32), chosen_small[4], column_start, 0
    )
    small_out = (
        lax.psum_scatter(chosen_small[0], ("dp", "tensor"), scatter_dimension=0, tiled=True),
        lax.psum_scatter(chosen_small[1], ("dp", "tensor"), scatter_dimension=0, tiled=True),
        lax.psum_scatter(chosen_small[2], ("dp", "tensor"), scatter_dimension=0, tiled=True),
        lax.psum_scatter(uprank_full, ("dp", "tensor"), scatter_dimension=1, tiled=True),
        lax.psum_scatter(bias_full, ("dp", "tensor"), scatter_dimension=0, tiled=True),
        lax.psum_scatter(chosen_small[5], ("dp", "tensor"), scatter_dimension=0, tiled=True),
    )
    chosen_big = jax.tree.map(pick, early_big, late_big)
    big_out = (
        lax.psum_scatter(
            chosen_big[0].astype(jnp.bfloat16), "dp", scatter_dimension=0, tiled=True
        ).astype(jnp.float32),
        lax.psum_scatter(
            chosen_big[1].astype(jnp.bfloat16), "dp", scatter_dimension=0, tiled=True
        ).astype(jnp.float32),
        lax.psum_scatter(
            chosen_big[2].astype(jnp.bfloat16), "dp", scatter_dimension=0, tiled=True
        ).astype(jnp.float32),
        lax.psum_scatter(
            chosen_big[3].astype(jnp.bfloat16), "dp", scatter_dimension=0, tiled=True
        ).astype(jnp.float32),
        lax.psum_scatter(
            chosen_big[4].astype(jnp.bfloat16), "dp", scatter_dimension=1, tiled=True
        ).astype(jnp.float32),
        lax.psum_scatter(
            chosen_big[5].astype(jnp.bfloat16), "dp", scatter_dimension=0, tiled=True
        ).astype(jnp.float32),
        lax.psum_scatter(
            chosen_big[6].astype(jnp.bfloat16), "dp", scatter_dimension=0, tiled=True
        ).astype(jnp.float32),
        lax.psum_scatter(
            chosen_big[7].astype(jnp.bfloat16), "dp", scatter_dimension=1, tiled=True
        ).astype(jnp.float32),
    )
    return (
        lifted(section_out),
        lifted(input_grad),
        lifted(small_out[0]),
        lifted(big_out[0]),
        lifted(big_out[1]),
        lifted(big_out[2]),
        lifted(big_out[3]),
        lifted(small_out[2]),
        lifted(small_out[3]),
        lifted(small_out[4]),
        lifted(small_out[5]),
        lifted(big_out[4]),
        lifted(small_out[1]),
        lifted(big_out[5]),
        lifted(big_out[6]),
        lifted(big_out[7]),
    )


def solution(mesh):
    placed = (
        P(("dp", "tensor"), None),
        P("dp"),
        P("section", ("dp", "tensor")),
        P("section", "dp", "tensor"),
        P("section", "dp", "tensor"),
        P("section", "dp", "tensor"),
        P("section", "dp", "tensor"),
        P("section", ("dp", "tensor"), None),
        P("section", None, ("dp", "tensor")),
        P("section", ("dp", "tensor")),
        P("section", ("dp", "tensor")),
        P("section", "tensor", "dp"),
        P("section", ("dp", "tensor")),
        P("section", "dp", "tensor"),
        P("section", "dp", "tensor"),
        P("section", "tensor", "dp"),
        P(("dp", "tensor"), None),
    )
    return jax.shard_map(
        shards,
        mesh=mesh,
        in_specs=placed,
        out_specs=(
            P("section", ("dp", "tensor"), None),
            P("section", ("dp", "tensor"), None),
            P("section", ("dp", "tensor")),
            P("section", "dp", "tensor"),
            P("section", "dp", "tensor"),
            P("section", "dp", "tensor"),
            P("section", "dp", "tensor"),
            P("section", ("dp", "tensor"), None),
            P("section", None, ("dp", "tensor")),
            P("section", ("dp", "tensor")),
            P("section", ("dp", "tensor")),
            P("section", "tensor", "dp"),
            P("section", ("dp", "tensor")),
            P("section", "dp", "tensor"),
            P("section", "dp", "tensor"),
            P("section", "tensor", "dp"),
        ),
        check_vma=False,
    )
```

profile of v0, /device:TPU:0, one launch (start us, length us, event | category | flops | bytes accessed | tf_op | source)
XLA Modules:
  0.0 2057.5 jit_solution(13290223647553488784)
XLA Ops:
  16.2 79.1 %all-reduce.13 = (f32[1024]{0:T(1024)S(1)}, f32[512]{0:T(512)S(1)}, f32[256]{0:T(256)}, f32[1024]{0:T(1024)S(1)}) all-reduce(f32[1024]{0:T(1024)S(1)} %bitcast_dynamic-update-slice_fusion.11, f32[512]{0:T(512)S(1)} %bitcast_dynamic-update-slice_fusion.10, ...), channel_id=2, replica_groups=mesh['section'=2,'dp'=8,'tensor'=2] {'dp','tensor'}, use_global_device_ids=true, to_apply=%add.2 | all-reduce | flops 2816 | bytes 22528
  105.4 38.3 %all-gather.2 = f32[1,1024,16]{2,0,1:T(1,128)S(1)} all-gather(f32[1,64,16]{2,0,1:T(1,128)S(1)} %copy.188), channel_id=4, replica_groups=mesh['section'=2,'dp'=8,'tensor'=2] {'dp','tensor'}, dimensions={1}, use_global_device_ids=true | all-gather | bytes 69632 | tf_op jit(solution)/shard_map/all_gather | solution.py:437
  143.8 39.2 %all-gather.3 = f32[1,16,512]{1,0,2:T(1,128)S(1)} all-gather(f32[1,16,32]{1,0,2:T(1,128)S(1)} %copy.189), channel_id=5, replica_groups=mesh['section'=2,'dp'=8,'tensor'=2] {'dp','tensor'}, dimensions={2}, use_global_device_ids=true | all-gather | bytes 34816 | tf_op jit(solution)/shard_map/all_gather | solution.py:438
  185.4 31.3 %all-gather.1 = bf16[1,1024,256]{2,1,0:T(8,128)(2,1)S(1)} all-gather(bf16[1,128,256]{2,1,0:T(8,128)(2,1)S(1)} %copy-done.114), channel_id=3, replica_groups=mesh['section'=2,'dp'=8,'tensor'=2] {'dp'}, dimensions={1}, use_global_device_ids=true | all-gather | bytes 589824 | tf_op jit(solution)/shard_map/all_gather | solution.py:426
  244.5 32.1 %all-gather.10 = bf16[1,1024,256]{2,1,0:T(8,128)(2,1)S(1)} all-gather(bf16[1,128,256]{2,1,0:T(8,128)(2,1)S(1)} %copy-done.115), channel_id=12, replica_groups=mesh['section'=2,'dp'=8,'tensor'=2] {'dp'}, dimensions={1}, use_global_device_ids=true | all-gather | bytes 589824 | tf_op jit(solution)/shard_map/all_gather | solution.py:425
  279.9 18.9 all-reduce.14
  300.7 39.5 %while.184 = (s32[]{:T(128)}, f32[2,128,256]{2,1,0:T(8,128)S(1)}, f32[1]{0:T(128)}, s32[]{:T(128)}, bf16[8,2,128,256]{3,2,1,0:T(8,128)(2,1)}, /*index=5*/bf16[8,...) while((s32[]{:T(128)}, f32[2,128,256]{2,1,0:T(8,128)S(1)}, ...), condition=%wide.region_4.5_spmd.clone, body=%wide.region_3.4_spmd.clone.sunk | while | flops 328205 | bytes 658154 | solution.py:38
  340.3 43.9 %while.180 = (s32[]{:T(128)}, f32[2,128,256]{2,1,0:T(8,128)S(1)}, f32[]{:T(128)}, f32[4,2,64,256]{3,2,0,1:T(8,128)S(1)}, f32[4,64]{1,0:T(4,128)}, /*index=5*/f32...) while((s32[]{:T(128)}, f32[2,128,256]{2,1,0:T(8,128)S(1)}, ...), condition=%wide.region_8.9_spmd.clone, body=%wide.region_5.8_spmd.clone.sunk | while | flops 133403008 | bytes 2542459 | solution.py:151
  415.9 49.2 %all-gather.41.cloned.1.call-done = bf16[1,1024,1408]{2,1,0:T(8,128)(2,1)} async-done(((bf16[1,128,1408]{2,1,0:T(8,128)(2,1)}), bf16[1,1024,1408]{2,1,0:T(8,128)(2,1)}) %all-gather.41.cloned.1.call-update) | async-done | bytes 2883600 | tf_op jit(solution)/shard_map/all_gather | solution.py:430
  469.1 54.2 %all-gather.43.cloned.1.call-done = bf16[1,1024,1408]{2,1,0:T(8,128)(2,1)} async-done(((bf16[1,128,1408]{2,1,0:T(8,128)(2,1)}), bf16[1,1024,1408]{2,1,0:T(8,128)(2,1)}) %all-gather.43.cloned.1.call-update) | async-done | bytes 2883600 | tf_op jit(solution)/shard_map/all_gather | solution.py:431
  527.7 55.9 %all-gather.45.cloned.1.call-done = bf16[1,1408,1024]{2,1,0:T(8,128)(2,1)} async-done(((bf16[1,1408,128]{2,1,0:T(8,128)(2,1)}), bf16[1,1408,1024]{2,1,0:T(8,128)(2,1)}) %all-gather.45.cloned.1.call-update) | async-done | bytes 2883600 | tf_op jit(solution)/shard_map/all_gather | solution.py:432
  587.4 18.7 reduce-scatter.29.cloned.1.call-done
  638.4 20.5 all-gather.19
  677.6 34.3 %while.185 = (s32[]{:T(128)}, f32[2,128,256]{2,1,0:T(8,128)S(1)}, f32[1]{0:T(128)}, s32[]{:T(128)}, bf16[8,2,128,256]{3,2,1,0:T(8,128)(2,1)}, /*index=5*/bf16[8,...) while((s32[]{:T(128)}, f32[2,128,256]{2,1,0:T(8,128)S(1)}, ...), condition=%wide.region_17.18_spmd.clone, body=%wide.region_16.17_spmd.clone.sunk | while | flops 328205 | bytes 658154 | solution.py:38
  712.6 61.3 %while.181 = (s32[]{:T(128)}, f32[2,128,256]{2,1,0:T(8,128)S(1)}, f32[]{:T(128)}, f32[4,2,64,256]{3,2,0,1:T(8,128)S(1)}, f32[4,64]{1,0:T(4,128)}, /*index=5*/f32...) while((s32[]{:T(128)}, f32[2,128,256]{2,1,0:T(8,128)S(1)}, ...), condition=%wide.region_21.22_spmd.clone, body=%wide.region_18.21_spmd.clone.sunk | while | flops 133403008 | bytes 2540959 | solution.py:151
  857.8 33.3 %while.178 = (s32[]{:T(128)}, f32[2,128,256]{2,1,0:T(8,128)S(1)}, f32[]{:T(128)}, f32[4,2,128,256]{3,2,1,0:T(8,128)}, f32[4]{0:T(128)}, /*index=5*/f32[4,64]{1,0...) while((s32[]{:T(128)}, f32[2,128,256]{2,1,0:T(8,128)S(1)}, ...), condition=%wide.region_33.34_spmd, body=%wide.region_31.33_spmd.sunk | while | flops 51544384 | bytes 1581607 | solution.py:151
  895.0 38.9 %while.186 = (s32[]{:T(128)}, f32[2,128,256]{2,1,0:T(8,128)S(1)}, f32[1]{0:T(128)}, s32[]{:T(128)}, bf16[8,2,128,256]{3,2,1,0:T(8,128)(2,1)}, /*index=5*/bf16[8,...) while((s32[]{:T(128)}, f32[2,128,256]{2,1,0:T(8,128)S(1)}, ...), condition=%wide.region_30.31_spmd.clone, body=%wide.region_29.30_spmd.clone.sunk | while | flops 328209 | bytes 658216 | solution.py:62
  935.3 101.7 %while.182 = (s32[]{:T(128)}, f32[2,128,256]{2,1,0:T(8,128)S(1)}, bf16[4,2,64,128]{3,2,0,1:T(8,128)(2,1)}, bf16[4,2,64,128]{3,2,0,1:T(8,128)(2,1)}, bf16[4,2,64,...) while((s32[]{:T(128)}, f32[2,128,256]{2,1,0:T(8,128)S(1)}, ...), condition=%wide.region_44.45_spmd.clone, body=%wide.region_34.44_spmd.clone.sunk | while | flops 272224896 | bytes 7115124 | solution.py:151
  1073.4 20.7 %reduce-scatter.33.cloned.1.call-done = f32[128,1024]{1,0:T(8,128)} async-done(((f32[256,1024]{1,0:T(8,128)}), f32[128,1024]{1,0:T(8,128)}) %reduce-scatter.33.cloned.1.call-update) | async-done | bytes 524304 | tf_op jit(solution)/shard_map/reduce_scatter | solution.py:184
  1150.4 29.6 %while.179 = (s32[]{:T(128)}, f32[2,128,256]{2,1,0:T(8,128)S(1)}, f32[]{:T(128)}, f32[4,2,128,256]{3,2,1,0:T(8,128)}, f32[4]{0:T(128)}, /*index=5*/f32[4,64]{1,0...) while((s32[]{:T(128)}, f32[2,128,256]{2,1,0:T(8,128)S(1)}, ...), condition=%wide.region_54.55_spmd, body=%wide.region_52.54_spmd.sunk | while | flops 51544384 | bytes 1582055 | solution.py:151
  1189.2 39.5 %while.187 = (s32[]{:T(128)}, f32[2,128,256]{2,1,0:T(8,128)S(1)}, f32[1]{0:T(128)}, s32[]{:T(128)}, bf16[8,2,128,256]{3,2,1,0:T(8,128)(2,1)}, /*index=5*/bf16[8,...) while((s32[]{:T(128)}, f32[2,128,256]{2,1,0:T(8,128)S(1)}, ...), condition=%wide.region_51.52_spmd.clone, body=%wide.region_50.51_spmd.clone.sunk | while | flops 328209 | bytes 658216 | solution.py:62
  1230.1 89.5 %while.183 = (s32[]{:T(128)}, f32[2,128,256]{2,1,0:T(8,128)S(1)}, bf16[4,2,64,128]{3,2,0,1:T(8,128)(2,1)}, bf16[4,2,64,128]{3,2,0,1:T(8,128)(2,1)}, bf16[4,2,64,...) while((s32[]{:T(128)}, f32[2,128,256]{2,1,0:T(8,128)S(1)}, ...), condition=%wide.region_65.66_spmd.clone, body=%wide.region_55.65_spmd.clone.sunk | while | flops 272224896 | bytes 7115408 | solution.py:151
  1372.0 31.1 %reduce-scatter.57.cloned.1.call-done = f32[32,16]{1,0:T(8,128)} async-done(((f32[512,16]{1,0:T(8,128)}), f32[32,16]{1,0:T(8,128)}) %reduce-scatter.57.cloned.1.call-update) | async-done | bytes 2064
  1404.5 74.7 %reduce-scatter.55.cloned.1.call-done = f32[64,16]{1,0:T(8,128)} async-done(((f32[1024,16]{1,0:T(8,128)}), f32[64,16]{1,0:T(8,128)}) %reduce-scatter.55.cloned.1.call-update) | async-done | bytes 4112
  1480.6 62.3 %reduce-scatter.59.cloned.1.call-done = bf16[128,512]{1,0:T(8,128)(2,1)} async-done(((bf16[1024,512]{1,0:T(8,128)(2,1)}), bf16[128,512]{1,0:T(8,128)(2,1)}) %reduce-scatter.59.cloned.1.call-update) | async-done | bytes 131088
  1544.7 64.8 %reduce-scatter.49.cloned.1.call-done = bf16[128,512]{1,0:T(8,128)(2,1)} async-done(((bf16[1024,512]{1,0:T(8,128)(2,1)}), bf16[128,512]{1,0:T(8,128)(2,1)}) %reduce-scatter.49.cloned.1.call-update) | async-done | bytes 131088 | tf_op jit(solution)/shard_map/reduce_scatter | solution.py:493
  1627.2 75.9 %all-reduce.12 = (f32[1024]{0:T(1024)S(1)}, f32[512]{0:T(512)S(1)}, f32[256]{0:T(256)S(1)}, f32[1024]{0:T(1024)S(1)}) all-reduce(f32[1024]{0:T(1024)S(1)} %broadcast_select_fusion.5, f32[512]{0:T(512)S(1)} %select_dynamic-update-slice_fusion, ...), channel_id=32, replica_groups=mesh['section'=2,'dp'=8,'tensor'=2] {'dp','tensor'}, use_global_device_ids=true, to_apply=%region_70.71.clone | all-reduce | flops 2816 | bytes 22528
  1706.3 50.6 %reduce-scatter.43.cloned.1.call-done = bf16[128,256]{1,0:T(8,128)(2,1)} async-done(((bf16[1024,256]{1,0:T(8,128)(2,1)}), bf16[128,256]{1,0:T(8,128)(2,1)}) %reduce-scatter.43.cloned.1.call-update) | async-done | bytes 65552 | tf_op jit(solution)/shard_map/reduce_scatter | solution.py:484
  1760.5 62.9 %reduce-scatter.47.cloned.1.call-done = bf16[128,512]{1,0:T(8,128)(2,1)} async-done(((bf16[1024,512]{1,0:T(8,128)(2,1)}), bf16[128,512]{1,0:T(8,128)(2,1)}) %reduce-scatter.47.cloned.1.call-update) | async-done | bytes 131088 | tf_op jit(solution)/shard_map/reduce_scatter | solution.py:490
  1825.1 73.0 %reduce-scatter.61.cloned.1.call-done = bf16[128,1408]{1,0:T(8,128)(2,1)} async-done(((bf16[1024,1408]{1,0:T(8,128)(2,1)}), bf16[128,1408]{1,0:T(8,128)(2,1)}) %reduce-scatter.61.cloned.1.call-update) | async-done | bytes 360464
  1900.2 72.8 %reduce-scatter.53.cloned.1.call-done = bf16[128,1408]{1,0:T(8,128)(2,1)} async-done(((bf16[1024,1408]{1,0:T(8,128)(2,1)}), bf16[128,1408]{1,0:T(8,128)(2,1)}) %reduce-scatter.53.cloned.1.call-update) | async-done | bytes 360464 | tf_op jit(solution)/shard_map/reduce_scatter | solution.py:502
  1974.9 73.4 %reduce-scatter.51.cloned.1.call-done = bf16[128,1408]{1,0:T(8,128)(2,1)} async-done(((bf16[1024,1408]{1,0:T(8,128)(2,1)}), bf16[128,1408]{1,0:T(8,128)(2,1)}) %reduce-scatter.51.cloned.1.call-update) | async-done | bytes 360464 | tf_op jit(solution)/shard_map/reduce_scatter | solution.py:499
  (1149 shorter events, 817.6 us)
Async XLA Ops:
  7.2 213.8 %all-gather.33.cloned.1.call-start = ((), (), s32[]{:S(2)}) async-start(), calls=%async_computation.32 | async-start | bytes 1179648 | tf_op jit(solution)/shard_map/all_gather | solution.py:427
  7.9 291.0 %all-gather.37.cloned.1.call-start = ((), (), s32[]{:S(2)}) async-start(), calls=%async_computation.34 | async-start | bytes 1179648 | tf_op jit(solution)/shard_map/all_gather | solution.py:428
  8.7 292.0 %all-gather.35.cloned.1.call-start = ((), (), s32[]{:S(2)}) async-start(), calls=%async_computation.33 | async-start | bytes 1179648 | tf_op jit(solution)/shard_map/all_gather | solution.py:21
  183.1 441.2 %copy-start.85 = (f32[1,16,256]{1,0,2:T(1,128)}, f32[1,16,256]{1,0,2:T(1,128)S(1)}, u32[]{:S(2)}) copy-start(f32[1,16,256]{1,0,2:T(1,128)S(1)} %constant_dynamic-slice_fusion.18) | copy-start | bytes 49156
  224.1 162.0 %all-gather.39.cloned.1.call-start = ((), (), s32[]{:S(2)}) async-start(), calls=%async_computation.35 | async-start | bytes 1179648 | tf_op jit(solution)/shard_map/all_gather | solution.py:429
  224.7 181.1 %reduce-scatter.27.cloned.1.call-start = ((), (), s32[]{:S(2)}) async-start(), calls=%async_computation.18 | async-start | bytes 1572864 | tf_op jit(solution)/shard_map/reduce_scatter | solution.py:184
  388.9 76.3 %all-gather.41.cloned.1.call-start = ((), (), s32[]{:S(2)}) async-start(), calls=%async_computation.36 | async-start | bytes 3244032 | tf_op jit(solution)/shard_map/all_gather | solution.py:430
  389.5 133.8 %all-gather.43.cloned.1.call-start = ((), (), s32[]{:S(2)}) async-start(), calls=%async_computation.37 | async-start | bytes 3244032 | tf_op jit(solution)/shard_map/all_gather | solution.py:431
  390.2 193.3 %all-gather.45.cloned.1.call-start = ((), (), s32[]{:S(2)}) async-start(), calls=%async_computation.38 | async-start | bytes 3244032 | tf_op jit(solution)/shard_map/all_gather | solution.py:432
  391.0 215.2 %reduce-scatter.29.cloned.1.call-start = ((), (), s32[]{:S(2)}) async-start(), calls=%async_computation.19 | async-start | bytes 1572864 | tf_op jit(solution)/shard_map/reduce_scatter | solution.py:184
  587.4 90.2 %all-gather.47.cloned.1.call-start = ((), (), s32[]{:S(2)}) async-start(), calls=%async_computation.39 | async-start | bytes 1179648 | tf_op jit(solution)/shard_map/all_gather | solution.py:21
  607.2 3.1 collective-permute-start
  637.2 163.6 %reduce-scatter.31.cloned.1.call-start = ((), (), s32[]{:S(2)}) async-start(), calls=%async_computation.20 | async-start | bytes 1572864 | tf_op jit(solution)/shard_map/reduce_scatter | solution.py:184
  780.1 51.8 %reduce-scatter.35.cloned.1.call-start = ((), (), s32[]{:S(2)}) async-start(), calls=%async_computation.22 | async-start | bytes 786432 | tf_op jit(solution)/shard_map/reduce_scatter | solution.py:192
  818.3 76.6 %all-gather.49.cloned.1.call-start = ((), (), s32[]{:S(2)}) async-start(), calls=%async_computation.40 | async-start | bytes 1179648 | tf_op jit(solution)/shard_map/all_gather | solution.py:44
  847.4 224.2 %reduce-scatter.37.cloned.1.call-start = ((), (), s32[]{:S(2)}) async-start(), calls=%async_computation.23 | async-start | bytes 786432 | tf_op jit(solution)/shard_map/reduce_scatter | solution.py:192
  1056.8 37.3 %reduce-scatter.33.cloned.1.call-start = ((), (), s32[]{:S(2)}) async-start(), calls=%async_computation.21 | async-start | bytes 1572864 | tf_op jit(solution)/shard_map/reduce_scatter | solution.py:184
  1061.0 70.5 %reduce-scatter.39.cloned.1.call-start = ((), (), s32[]{:S(2)}) async-start(), calls=%async_computation.24 | async-start | bytes 786432 | tf_op jit(solution)/shard_map/reduce_scatter | solution.py:192
  1097.0 3.4 collective-permute-start.1
  1116.7 72.5 %all-gather.51.cloned.1.call-start = ((), (), s32[]{:S(2)}) async-start(), calls=%async_computation.41 | async-start | bytes 1179648 | tf_op jit(solution)/shard_map/all_gather | solution.py:44
  1148.8 254.3 %reduce-scatter.57.cloned.1.call-start = ((), (), s32[]{:S(2)}) async-start(), calls=%async_computation.43 | async-start | bytes 278528
  1327.2 152.0 %reduce-scatter.55.cloned.1.call-start = ((), (), s32[]{:S(2)}) async-start(), calls=%async_computation.42 | async-start | bytes 557056
  1328.9 214.0 %reduce-scatter.59.cloned.1.call-start = ((), (), s32[]{:S(2)}) async-start(), calls=%async_computation.44 | async-start | bytes 1179648
  1332.8 276.8 %reduce-scatter.49.cloned.1.call-start = ((), (), s32[]{:S(2)}) async-start(), calls=%async_computation.29 | async-start | bytes 1179648 | tf_op jit(solution)/shard_map/reduce_scatter | solution.py:493
  1335.2 290.7 %reduce-scatter.41.cloned.1.call-start = ((), (), s32[]{:S(2)}) async-start(), calls=%async_computation.25 | async-start | bytes 786432 | tf_op jit(solution)/shard_map/reduce_scatter | solution.py:192
  1346.2 358.6 %reduce-scatter.45.cloned.1.call-start = ((), (), s32[]{:S(2)}) async-start(), calls=%async_computation.27 | async-start | bytes 589824 | tf_op jit(solution)/shard_map/reduce_scatter | solution.py:487
  1347.9 409.0 %reduce-scatter.43.cloned.1.call-start = ((), (), s32[]{:S(2)}) async-start(), calls=%async_computation.26 | async-start | bytes 589824 | tf_op jit(solution)/shard_map/reduce_scatter | solution.py:484
  1349.5 473.9 %reduce-scatter.47.cloned.1.call-start = ((), (), s32[]{:S(2)}) async-start(), calls=%async_computation.28 | async-start | bytes 1179648 | tf_op jit(solution)/shard_map/reduce_scatter | solution.py:490
  1351.6 546.5 %reduce-scatter.61.cloned.1.call-start = ((), (), s32[]{:S(2)}) async-start(), calls=%async_computation.45 | async-start | bytes 3244032
  1360.0 613.1 %reduce-scatter.53.cloned.1.call-start = ((), (), s32[]{:S(2)}) async-start(), calls=%async_computation.31 | async-start | bytes 3244032 | tf_op jit(solution)/shard_map/reduce_scatter | solution.py:502
  1364.9 683.4 %reduce-scatter.51.cloned.1.call-start = ((), (), s32[]{:S(2)}) async-start(), calls=%async_computation.30 | async-start | bytes 3244032 | tf_op jit(solution)/shard_map/reduce_scatter | solution.py:499
  1369.7 388.7 %copy-start.75 = (bf16[128,1024]{1,0:T(8,128)(2,1)S(1)}, bf16[128,1024]{1,0:T(8,128)(2,1)}, u32[]{:S(2)}) copy-start(bf16[128,1024]{1,0:T(8,128)(2,1)} %copy-done.74) | copy-start | bytes 786436
  (169 other events, 4636.3 us)
Sparse Core Ops, SparseCore 0:
  10.1 43.1 all-gather.32
  55.4 39.1 all-gather.36
  224.2 37.5 all-gather.34
  263.7 38.4 all-gather.38
  389.0 16.7 reduce-scatter.26
  407.9 57.2 all-gather.40
  467.4 55.9 all-gather.42
  525.3 58.1 all-gather.44
  587.5 18.5 reduce-scatter.28
  637.4 40.2 all-gather.46
  780.2 20.6 reduce-scatter.30
  818.5 13.3 reduce-scatter.34
  847.5 40.2 all-gather.48
  1056.9 14.6 reduce-scatter.36
  1073.7 20.3 reduce-scatter.32
  1116.8 14.6 reduce-scatter.38
  1148.9 40.2 all-gather.50
  1327.3 75.7 reduce-scatter.56
  1405.3 73.7 reduce-scatter.54
  1482.4 60.4 reduce-scatter.58
  1546.3 63.1 reduce-scatter.48
  1612.3 13.5 reduce-scatter.40
  1629.3 62.6 reduce-scatter.44
  1695.2 61.6 reduce-scatter.42
  1760.3 63.0 reduce-scatter.46
  1826.9 71.2 reduce-scatter.60
  1901.5 71.4 reduce-scatter.52
  1976.6 71.6 reduce-scatter.50
where the time goes:
time: 2080 us; the launch traced here: 2060 us
  waiting for transfers between devices  859 us (41%)
  blocking collectives  424 us (20%)
  other arithmetic  243 us (12%)
  local copies, waits for them, and re-layouts  203 us (10%)
  matrix products  176 us (8%)
  loops' own time  116 us (6%)
  between operations  23.5 us (1%)
    unnamed x32, waiting for transfers between devices  245 us
    unnamed x3, blocking collectives  174 us
    dot_general x48, matrix products, product(): return jnp.dot(left, right, preferred_element_type=jnp.float32)  85.1 us
    reduce_scatter x1, waiting for transfers between devices, shards(): lax.psum_scatter(chosen_big[5].astype(jnp.bfloat16), 'dp', scatter_dimens...  73.4 us
    reduce_scatter x1, waiting for transfers between devices, shards(): lax.psum_scatter(chosen_big[6].astype(jnp.bfloat16), 'dp', scatter_dimens...  72.8 us
    reduce_scatter x1, waiting for transfers between devices, shards(): lax.psum_scatter(chosen_big[3].astype(jnp.bfloat16), 'dp', scatter_dimens...  64.8 us
    reduce_scatter x1, waiting for transfers between devices, shards(): lax.psum_scatter(chosen_big[2].astype(jnp.bfloat16), 'dp', scatter_dimens...  62.9 us
    reduce_scatter x4, waiting for transfers between devices, scatter_rows(): return lax.psum_scatter(values, 'tensor', scatter_dimension=0, tiled=True)  57.6 us
  transfers between devices with their start and end apart: 30, of which 24 were waited for; matrix products, arithmetic and copies ran while one was open for 11% of the time, Pallas kernels for 0%

commit v1 on v0

v1 whole, which is shorter than its diff:
```python
import functools

import jax
import jax.numpy as jnp
from jax import lax
from jax.experimental import pallas as pl
from jax.experimental.pallas import tpu as pltpu
from jax.sharding import PartitionSpec as P

HEADS = 4
KDIM = 128
VDIM = 256
RANK = 16
SUB = 16
PACK = 128
STATE_PAD = 16

norm_eps = 1e-06
head_eps = 1e-05
f32 = jnp.float32
bf16 = jnp.bfloat16
INTERPRET = False


def swap(block, axis):
    return lax.ppermute(block, axis, [(0, 1), (1, 0)])


def mm(left, right, dims):
    return lax.dot_general(left, right, (dims, ((), ())), preferred_element_type=f32)


def exact(left, right, dims=((1,), (0,))):
    return lax.dot_general(
        left, right, (dims, ((), ())), precision=lax.Precision.HIGHEST, preferred_element_type=f32
    )


NN = ((1,), (0,))
NT = ((1,), (1,))
TN = ((0,), (0,))


def call(body, outs, *args):
    return pl.pallas_call(
        body,
        out_shape=[jax.ShapeDtypeStruct(shape, kind) for shape, kind in outs],
        interpret=INTERPRET,
    )(*args)


def iota2(rows, cols, axis):
    return lax.broadcasted_iota(jnp.int32, (rows, cols), axis)


def lower(count):
    return jnp.where(iota2(count, count, 0) >= iota2(count, count, 1), 1.0, 0.0)


def levels(count):
    half, out = count // 2, []
    while half >= SUB:
        out.append(half)
        half //= 2
    return out


def level_factors(sums, half):
    count, width = sums.shape
    parts = sums.reshape(count // (2 * half), 2 * half, width)
    middle = jnp.broadcast_to(parts[:, half - 1 : half, :], parts.shape).reshape(count, width)
    late = (iota2(count, width, 0) & half) != 0
    gap = sums - middle
    to_late = jnp.where(late, jnp.exp(jnp.minimum(gap, 0.0)), 0.0)
    to_early = jnp.where(late, 0.0, jnp.exp(jnp.minimum(-gap, 0.0)))
    return to_late, to_early


def level_mask(count, half):
    rows, cols = iota2(count, count, 0), iota2(count, count, 1)
    bits = 2 * half - 1
    return (rows & ~bits) == (cols & ~bits)


def pair_mask(seg_col, seg_row, count):
    same = seg_col == seg_row
    return same & (iota2(count, count, 0) >= iota2(count, count, 1))


def pick_mask(count, offset):
    rows, cols = iota2(count, count, 0), iota2(count, count, 1)
    return cols == ((rows & ~(SUB - 1)) + offset)


def sub_factor(sums3, offset):
    return jnp.exp(jnp.minimum(sums3 - sums3[:, offset : offset + 1, :], 0.0))


def pre_body(
    proj, up3, bias, seg_col, seg_before, logits_o, sums_o, open_o, keep_o, end_o, through_o, pack_o
):
    count = proj.shape[0]
    logits = exact(proj[:, 768:896], up3[...]) + bias[...]
    decay = (jnp.minimum(logits, 0.0) - jnp.log1p(jnp.exp(-jnp.abs(logits)))) / 16.0
    sums = exact(lower(count), decay)
    last = sums[count - 1 : count, :]
    seg = seg_col[...]
    seg_last = seg[count - 1 : count, :]
    before = seg_before[...]
    opened = jnp.where(seg == before, proj[:, 0:128] * jnp.exp(sums), 0.0)
    kept = jnp.where(seg == seg_last, proj[:, 128:256] * jnp.exp(last - sums), 0.0)
    state = exact(proj[:, 256:512], kept, TN)
    through = jnp.where(before == seg_last, jnp.exp(last), 0.0)
    logits_o[...] = logits
    sums_o[...] = sums
    open_o[...] = opened
    keep_o[...] = kept
    end_o[...] = state
    through_o[...] = through
    pack_o[0:VDIM, :] = state.astype(bf16)
    pack_o[VDIM : VDIM + STATE_PAD, :] = jnp.broadcast_to(through, (STATE_PAD, KDIM)).astype(bf16)


def within_body(proj, sums_r, seg_col, seg_row, scores_o, out_o):
    count = proj.shape[0]
    query, key = proj[:, 0:128], proj[:, 128:256]
    sums = sums_r[...]
    scores = jnp.zeros((count, count), f32)
    for half in levels(count):
        to_late, to_early = level_factors(sums, half)
        part = exact(query * to_late, key * to_early, NT)
        scores = scores + jnp.where(level_mask(count, half), part, 0.0)
    blocks = (count // SUB, SUB, KDIM)
    query3, key3, sums3 = query.reshape(blocks), key.reshape(blocks), sums.reshape(blocks)
    for offset in range(SUB):
        weight = sub_factor(sums3, offset)
        column = jnp.sum(query3 * weight * key3[:, offset : offset + 1, :], axis=-1, keepdims=True)
        scores = jnp.where(pick_mask(count, offset), column.reshape(count, 1), scores)
    scores = jnp.where(pair_mask(seg_col[...], seg_row[...], count), scores, 0.0)
    scores_o[...] = scores
    out_o[...] = exact(scores, proj[:, 256:512])


def post_body(within, opened, state_in, proj, gain, unit_o, scale_o, branch_o):
    mixed = within[...] + exact(opened[...], state_in[...], NT)
    scale = lax.rsqrt(jnp.mean(mixed * mixed, axis=-1, keepdims=True) + head_eps)
    unit = mixed * scale
    gate = proj[:, 512:768]
    unit_o[...] = unit
    scale_o[...] = scale
    branch_o[...] = (unit * gain[...] * (gate * jax.nn.sigmoid(gate))).astype(bf16)


def head_back_body(
    branch_delta, unit_r, scale, proj, gain_r, opened, through, low_o, gain_o, mixed_o, pack_o
):
    delta, unit, gate, gain = branch_delta[...], unit_r[...], proj[:, 512:768], gain_r[...]
    sigma = jax.nn.sigmoid(gate)
    swish = gate * sigma
    slope = sigma * (1.0 + gate * (1.0 - sigma))
    low_o[...] = (delta * unit * gain * slope).astype(bf16)
    through_unit = delta * swish
    gain_o[...] = jnp.sum(through_unit * unit, axis=0, keepdims=True)
    inner = through_unit * gain
    mixed = scale[...] * (inner - unit * jnp.mean(inner * unit, axis=-1, keepdims=True))
    mixed_o[...] = mixed
    pack_o[0:VDIM, :] = exact(mixed, opened[...], TN).astype(bf16)
    pack_o[VDIM : VDIM + STATE_PAD, :] = jnp.broadcast_to(
        through[...], (STATE_PAD, KDIM)
    ).astype(bf16)


def within_back_body(
    mixed_r, proj, sums_r, scores, seg_col, seg_row, seg_before, state_in, query_o, key_o, value_o
):
    count = proj.shape[0]
    query, key, value = proj[:, 0:128], proj[:, 128:256], proj[:, 256:512]
    sums, mixed = sums_r[...], mixed_r[...]
    value_o[...] = exact(scores[...], mixed, TN)
    grad = jnp.where(
        pair_mask(seg_col[...], seg_row[...], count), exact(mixed, value, NT), 0.0
    )
    query_delta = jnp.where(
        seg_col[...] == seg_before[...], jnp.exp(sums) * exact(mixed, state_in[...]), 0.0
    )
    key_delta = jnp.zeros((count, KDIM), f32)
    for half in levels(count):
        to_late, to_early = level_factors(sums, half)
        part = jnp.where(level_mask(count, half), grad, 0.0)
        query_delta = query_delta + to_late * exact(part, key * to_early)
        key_delta = key_delta + to_early * exact(part, query * to_late, TN)
    blocks = (count // SUB, SUB, KDIM)
    query3, key3, sums3 = query.reshape(blocks), key.reshape(blocks), sums.reshape(blocks)
    place = lax.broadcasted_iota(jnp.int32, blocks, 1)
    query_sub, key_sub = jnp.zeros(blocks, f32), jnp.zeros(blocks, f32)
    for offset in range(SUB):
        weight = sub_factor(sums3, offset)
        column = jnp.sum(jnp.where(pick_mask(count, offset), grad, 0.0), axis=-1, keepdims=True)
        weighted = weight * column.reshape(count // SUB, SUB, 1)
        query_sub = query_sub + weighted * key3[:, offset : offset + 1, :]
        total = jnp.sum(weighted * query3, axis=1, keepdims=True)
        key_sub = jnp.where(place == offset, total, key_sub)
    query_o[...] = query_delta + query_sub.reshape(count, KDIM)
    key_o[...] = key_delta + key_sub.reshape(count, KDIM)


def state_back_body(
    query_d, key_d, value_d, state_grad, state_in, state_end, through, proj, sums_r, kept,
    logits, seg_col, up3, gate_low, low_o, up_o, bias_o,
):
    count = proj.shape[0]
    grad, sums = state_grad[...], sums_r[...]
    last = sums[count - 1 : count, :]
    seg = seg_col[...]
    query_delta = query_d[...]
    value_delta = value_d[...] + exact(kept[...], grad, NT)
    key_delta = key_d[...] + jnp.where(
        seg == seg[count - 1 : count, :],
        jnp.exp(last - sums) * exact(proj[:, 256:512], grad),
        0.0,
    )
    final = state_end[...] + through[...] * state_in[...]
    beyond = jnp.sum(final * grad, axis=0, keepdims=True)
    local = proj[:, 0:128] * query_delta - proj[:, 128:256] * key_delta
    decay_delta = exact(lower(count), local, TN) + beyond
    logit_delta = decay_delta * jax.nn.sigmoid(-logits[...]) / 16.0
    bias_o[...] = jnp.sum(logit_delta, axis=0, keepdims=True)
    ranks = exact(proj[:, 768:896], logit_delta, TN)
    up_o[...] = ranks[0:16, :] + ranks[16:32, :] + ranks[32:48, :]
    low_o[:, 0:128] = query_delta.astype(bf16)
    low_o[:, 128:256] = key_delta.astype(bf16)
    low_o[:, 256:512] = value_delta.astype(bf16)
    low_o[:, 512:768] = gate_low[...]
    low_o[:, 768:896] = exact(logit_delta, up3[...], NT).astype(bf16)


def scan_states(pack, backward):
    count = lax.axis_size("dp")
    here = lax.axis_index("dp")
    state = pack[:VDIM].astype(f32)
    through = pack[VDIM : VDIM + 1].astype(f32)
    carried, passed = jnp.zeros_like(state), jnp.ones_like(through)
    step = 1
    while step < count:
        other = lax.ppermute(pack, "dp", [(i, i ^ step) for i in range(count)])
        other_state = other[:VDIM].astype(f32)
        other_through = other[VDIM : VDIM + 1].astype(f32)
        mine_later = (here & step) != 0
        ahead = jnp.logical_not(mine_later) if backward else mine_later
        carried = jnp.where(ahead, carried + passed * other_state, carried)
        passed = jnp.where(ahead, passed * other_through, passed)
        state = jnp.where(ahead, state + through * other_state, other_state + other_through * state)
        through = through * other_through
        step *= 2
        if step < count:
            pack = jnp.concatenate(
                [state, jnp.broadcast_to(through, (STATE_PAD, KDIM))], axis=0
            ).astype(bf16)
    return carried


def gather_tokens(block, tensor_index, section_index):
    other = swap(block, "tensor")
    first = tensor_index == 0
    pair = jnp.stack([jnp.where(first, block, other), jnp.where(first, other, block)])
    far = swap(pair, "section")
    left = section_index == 0
    whole = jnp.stack([jnp.where(left, pair, far), jnp.where(left, far, pair)], axis=1)
    return whole.reshape(4 * block.shape[0], block.shape[1])


def scatter_tokens(partial, kind, tensor_index, section_index):
    rows = partial.shape[0] // 4
    parts = partial.reshape(2, 2, rows, partial.shape[1])
    left = section_index == 0
    keep = jnp.where(left, parts[:, 0], parts[:, 1])
    send = jnp.where(left, parts[:, 1], parts[:, 0])
    both = keep + swap(send, "section")
    first = tensor_index == 0
    mine = jnp.where(first, both[0], both[1])
    theirs = jnp.where(first, both[1], both[0]).astype(kind)
    return mine + swap(theirs, "tensor").astype(f32)


def rms_scale(values, epsilon):
    return lax.rsqrt(jnp.mean(values * values, axis=-1, keepdims=True) + epsilon)


def norm_back(grad_unit, unit_values, scale_values):
    return scale_values * (
        grad_unit - unit_values * jnp.mean(grad_unit * unit_values, axis=-1, keepdims=True)
    )


def layer_forward(layer_in, seg, params, where):
    attn, feed, small = params
    mixer_gain, feed_gain, up3, bias, head_gain = small
    seg_col, seg_row, seg_before = seg
    count = seg_col.shape[0]
    scale_one = rms_scale(layer_in, norm_eps)
    hidden_one = gather_tokens((layer_in * scale_one * mixer_gain).astype(bf16), *where)
    proj = mm(hidden_one, attn[:, :896], NN)
    wide, tall = (count, KDIM), (count, VDIM)
    logits, sums, opened, kept, state_end, through, pack = call(
        pre_body,
        [(wide, f32)] * 4
        + [((VDIM, KDIM), f32), ((1, KDIM), f32), ((VDIM + STATE_PAD, KDIM), bf16)],
        proj, up3, bias, seg_col, seg_before,
    )
    scores, within = call(
        within_body, [((count, count), f32), (tall, f32)], proj, sums, seg_col, seg_row
    )
    state_in = scan_states(pack, False)
    unit, scale_head, branch = call(
        post_body,
        [(tall, f32), ((count, 1), f32), (tall, bf16)],
        within, opened, state_in, proj, head_gain,
    )
    mid = layer_in + scatter_tokens(mm(branch, attn[:, 896:], NT), f32, *where)
    scale_two = rms_scale(mid, norm_eps)
    hidden_two = gather_tokens((mid * scale_two * feed_gain).astype(bf16), *where)
    units = feed.shape[1] // 3
    both = mm(hidden_two, feed[:, : 2 * units], NN)
    gate_pre, up_pre = both[:, :units], both[:, units:]
    inner = (jax.nn.silu(gate_pre) * up_pre).astype(bf16)
    result = mid + scatter_tokens(mm(inner, feed[:, 2 * units :], NT), f32, *where)
    saved = (
        layer_in, scale_one, hidden_one, proj, logits, sums, opened, kept, state_end, through,
        scores, state_in, unit, scale_head, branch, mid, scale_two, hidden_two, both, inner,
    )
    return result, saved


def layer_backward(saved, cotangent, seg, params, where):
    attn, feed, small = params
    mixer_gain, feed_gain, up3, bias, head_gain = small
    seg_col, seg_row, seg_before = seg
    (
        layer_in, scale_one, hidden_one, proj, logits, sums, opened, kept, state_end, through,
        scores, state_in, unit, scale_head, branch, mid, scale_two, hidden_two, both, inner,
    ) = saved
    count = seg_col.shape[0]
    wide, tall = (count, KDIM), (count, VDIM)
    units = feed.shape[1] // 3
    cot = gather_tokens(cotangent.astype(bf16), *where)
    inner_delta = mm(cot, feed[:, 2 * units :], NN)
    gate_pre, up_pre = both[:, :units], both[:, units:]
    sigma = jax.nn.sigmoid(gate_pre)
    gate_delta = inner_delta * up_pre * (sigma * (1.0 + gate_pre * (1.0 - sigma)))
    up_delta = inner_delta * (gate_pre * sigma)
    low_two = jnp.concatenate([gate_delta, up_delta], axis=1).astype(bf16)
    two_delta = mm(low_two, feed[:, : 2 * units], NT)
    feed_grad = jnp.concatenate(
        [mm(hidden_two, low_two, TN).astype(bf16), mm(cot, inner, TN).astype(bf16)], axis=1
    )
    feed_reduced = lax.psum_scatter(feed_grad, "dp", scatter_dimension=0, tiled=True)
    feed_gain_grad = jnp.sum(two_delta * hidden_two.astype(f32), axis=0) / feed_gain
    two_local = scatter_tokens(two_delta, bf16, *where)
    mid_delta = cotangent + norm_back(two_local * feed_gain, mid * scale_two, scale_two)
    mid_low = gather_tokens(mid_delta.astype(bf16), *where)
    branch_delta = mm(mid_low, attn[:, 896:], NN)
    gate_low, head_gain_grad, mixed_delta, pack = call(
        head_back_body,
        [(tall, bf16), ((1, VDIM), f32), (tall, f32), ((VDIM + STATE_PAD, KDIM), bf16)],
        branch_delta, unit, scale_head, proj, head_gain, opened, through,
    )
    query_d, key_d, value_d = call(
        within_back_body,
        [(wide, f32), (wide, f32), (tall, f32)],
        mixed_delta, proj, sums, scores, seg_col, seg_row, seg_before, state_in,
    )
    out_grad = mm(mid_low, branch, TN).astype(bf16)
    state_grad = scan_states(pack, True)
    low_one, up_grad, bias_grad = call(
        state_back_body,
        [((count, 896), bf16), ((RANK, KDIM), f32), ((1, KDIM), f32)],
        query_d, key_d, value_d, state_grad, state_in, state_end, through, proj, sums, kept,
        logits, seg_col, up3, gate_low,
    )
    one_delta = mm(low_one, attn[:, :896], NT)
    main_grad = mm(hidden_one, low_one, TN)
    mixer_gain_grad = jnp.sum(one_delta * hidden_one.astype(f32), axis=0) / mixer_gain
    depth = main_grad.shape[0]
    tensor_index, section_index = where
    head = tensor_index * 2 + section_index
    ranks = jnp.concatenate([up_grad.T, bias_grad.T, jnp.zeros((KDIM, 1), f32)], axis=1)
    ranks = lax.dynamic_update_slice(
        jnp.zeros((HEADS * KDIM, RANK + 2), f32), ranks, (head * KDIM, 0)
    ).reshape(depth, -1)
    repeat = depth // VDIM
    gains = jnp.broadcast_to(head_gain_grad.reshape(VDIM, 1), (VDIM, repeat)).reshape(depth, 1)
    smalls = jnp.concatenate(
        [main_grad[:, 768:784], mixer_gain_grad[:, None], feed_gain_grad[:, None], ranks, gains],
        axis=1,
    )
    smalls = jnp.pad(smalls, ((0, 0), (0, PACK - smalls.shape[1])))
    attn_grad = jnp.concatenate(
        [main_grad[:, :768].astype(bf16), smalls.astype(bf16), out_grad], axis=1
    )
    attn_reduced = lax.psum_scatter(attn_grad, "dp", scatter_dimension=0, tiled=True)
    one_local = scatter_tokens(one_delta, bf16, *where)
    input_delta = mid_delta + norm_back(one_local * mixer_gain, layer_in * scale_one, scale_one)
    return input_delta, attn_reduced, feed_reduced


def in_three(values):
    high = lax.reduce_precision(values, 8, 7)
    rest = values - high
    middle = lax.reduce_precision(rest, 8, 7)
    return [high.astype(bf16), middle.astype(bf16), (rest - middle).astype(bf16)]


def small_params(attn, tensor_index, section_index):
    depth = attn.shape[0]
    pack = attn[:, 768:896].astype(f32)
    rest = pack[:, 48:60] + pack[:, 60:72] + pack[:, 72:84]
    ranks = rest[:, 2:11].reshape(HEADS * KDIM, RANK + 2)
    head = tensor_index * 2 + section_index
    ranks = lax.dynamic_slice_in_dim(ranks, head * KDIM, KDIM, 0).T
    up = ranks[:RANK]
    up3 = jnp.concatenate([up, up, up, jnp.zeros((PACK - 3 * RANK, KDIM), f32)], axis=0)
    head_gain = rest[:, 11].reshape(VDIM, depth // VDIM)[:, 0]
    return rest[:, 0], rest[:, 1], up3, ranks[RANK : RANK + 1], head_gain[None]


def shards(
    inputs, segments, mixer_gain, query_weight, key_weight, value_weight, outgate_weight,
    decay_down, decay_up, decay_bias, head_gain, output_weight, feed_gain, gate_weight,
    up_weight, down_weight, cotangent,
):
    section_index = lax.axis_index("section")
    tensor_index = lax.axis_index("tensor")
    dp_index = lax.axis_index("dp")
    where = (tensor_index, section_index)
    left, first = section_index == 0, tensor_index == 0
    segment_ids = segments.astype(f32)
    count = segment_ids.shape[0]

    narrow = mixer_gain.shape[1]
    ranks = jnp.concatenate(
        [decay_up[0].T, decay_bias[0][:, None], jnp.zeros((decay_bias.shape[1], 1), f32)], axis=1
    ).reshape(narrow, -1)
    spread = narrow // head_gain.shape[1]
    gains = jnp.broadcast_to(head_gain[0][:, None], (head_gain.shape[1], spread)).reshape(narrow, 1)
    mine = jnp.concatenate(
        [decay_down[0], mixer_gain[0][:, None], feed_gain[0][:, None], ranks, gains], axis=1
    )
    theirs = swap(mine, "tensor")
    rows = jnp.concatenate([jnp.where(first, mine, theirs), jnp.where(first, theirs, mine)], axis=0)
    seg_end = jnp.broadcast_to(segment_ids[-1:][None], (2 * narrow, 1)).astype(bf16)
    pack = jnp.concatenate(in_three(rows[:, :RANK]) + in_three(rows[:, RANK:]) + [seg_end], axis=1)
    pack = jnp.pad(pack, ((0, 0), (0, PACK - pack.shape[1])))

    def half(weight, side):
        width = weight.shape[1] // 2
        return weight[:, side * width : (side + 1) * width]

    out_t, down_t = output_weight[0].T, down_weight[0].T

    def attn_half(side):
        parts = [half(w, side) for w in (query_weight[0], key_weight[0], value_weight[0], outgate_weight[0])]
        return jnp.concatenate(parts + [pack, half(out_t, side)], axis=1)

    def feed_half(side):
        parts = [half(w, side) for w in (gate_weight[0], up_weight[0], down_t)]
        return jnp.concatenate(parts, axis=1)

    def per_layer(side_zero, side_one):
        keep = jnp.where(left, side_zero, side_one)
        got = swap(jnp.where(left, side_one, side_zero), "section")
        return jnp.where(left, keep, got), jnp.where(left, got, keep)

    attn_parts = per_layer(attn_half(0), attn_half(1))
    feed_parts = per_layer(feed_half(0), feed_half(1))
    attn, feed = [], []
    for layer in range(2):
        attn.append(lax.all_gather(attn_parts[layer], "dp", axis=0, tiled=True))
        feed.append(lax.all_gather(feed_parts[layer], "dp", axis=0, tiled=True))
    params = [(attn[k], feed[k], small_params(attn[k], *where)) for k in range(2)]
    wide = 2 * narrow
    earlier = lax.dynamic_slice(
        attn[0], (jnp.maximum(dp_index - 1, 0) * wide, 768 + 84), (1, 1)
    ).astype(f32)
    seg_before = jnp.where(dp_index == 0, -1.0, earlier)
    seg = (segment_ids[:, None], segment_ids[None, :], seg_before)

    own = inputs.shape[0] // 2
    layer_in = lax.dynamic_slice_in_dim(inputs, section_index * own, own, 0)
    cot = lax.dynamic_slice_in_dim(cotangent, section_index * own, own, 0)
    out0, saved0 = layer_forward(layer_in, seg, params[0], where)
    out1, saved1 = layer_forward(out0, seg, params[1], where)
    delta1, attn_red1, feed_red1 = layer_backward(saved1, cot, seg, params[1], where)
    delta0, attn_red0, feed_red0 = layer_backward(saved0, delta1, seg, params[0], where)

    def to_section(of_zero, of_one):
        keep = jnp.where(left, of_zero, of_one)
        got = swap(jnp.where(left, of_one, of_zero), "section")
        return keep, got

    def joined(keep, got, axis):
        return jnp.concatenate([jnp.where(left, keep, got), jnp.where(left, got, keep)], axis=axis)

    section_out = joined(*to_section(out0, out1), 0)
    input_grad = joined(*to_section(delta0, delta1), 0)
    attn_keep, attn_got = to_section(attn_red0, attn_red1)
    feed_keep, feed_got = to_section(feed_red0, feed_red1)

    def columns(keep, got, start, width):
        return joined(keep[:, start : start + width], got[:, start : start + width], 1).astype(f32)

    units = feed_keep.shape[1] // 3
    small = attn_keep[:, 768:896].astype(f32) + attn_got[:, 768:896].astype(f32)
    small_mine = jnp.where(first, small[:narrow], small[narrow:])
    small_theirs = jnp.where(first, small[narrow:], small[:narrow])
    small = small_mine + swap(small_theirs, "tensor")
    ranks = small[:, 18:27].reshape(decay_bias.shape[1], RANK + 2)
    outs = (
        section_out,
        input_grad,
        small[:, 16],
        columns(attn_keep, attn_got, 0, 128),
        columns(attn_keep, attn_got, 128, 128),
        columns(attn_keep, attn_got, 256, 256),
        columns(attn_keep, attn_got, 512, 256),
        small[:, :16],
        ranks[:, :RANK].T,
        ranks[:, RANK],
        small[:, 27].reshape(-1, spread)[:, 0],
        columns(attn_keep, attn_got, 896, 256).T,
        small[:, 17],
        columns(feed_keep, feed_got, 0, units),
        columns(feed_keep, feed_got, units, units),
        columns(feed_keep, feed_got, 2 * units, units).T,
    )
    return tuple(out[None] for out in outs)


def solution(mesh):
    rows = P(("dp", "tensor"), None)
    vector = P("section", ("dp", "tensor"))
    down_in = P("section", "dp", "tensor")
    up_out = P("section", "tensor", "dp")
    placed = (
        rows, P("dp"), vector, down_in, down_in, down_in, down_in,
        P("section", ("dp", "tensor"), None), P("section", None, ("dp", "tensor")),
        vector, vector, up_out, vector, down_in, down_in, up_out, rows,
    )
    tokens = P("section", ("dp", "tensor"), None)
    return jax.shard_map(
        shards,
        mesh=mesh,
        in_specs=placed,
        out_specs=(
            tokens, tokens, vector, down_in, down_in, down_in, down_in, tokens,
            P("section", None, ("dp", "tensor")), vector, vector, up_out, vector,
            down_in, down_in, up_out,
        ),
        check_vma=False,
    )
```

time: 2080 us -> 797 us (0.38)
  blocking collectives: 424 us -> 0 us
  waiting for transfers between devices: 859 us -> 533 us
  other arithmetic: 243 us -> 60 us
  local copies, waits for them, and re-layouts: 203 us -> 49 us
  matrix products: 176 us -> 44.2 us
  loops' own time: 116 us -> 0 us
  Pallas kernels: 0 us -> 47.6 us
  starting transfers between devices: 13.1 us -> 42.6 us
    all_gather x14 -> x0, blocking collectives: 250 us -> none  [the longest x1 39.2 us: shards(): lax.all_gather(decay_up[0], ('dp', 'tensor'), axis=1, tiled=True)]
    unnamed x32 -> x8, waiting for transfers between devices: 245 us -> 0.81 us
    unnamed x3 -> x0, blocking collectives: 174 us -> none
    reduce_scatter x14 -> x4, waiting for transfers between devices: 432 us -> 280 us  [the longest x2 181 us: layer_backward(): lax.psum_scatter(feed_grad, 'dp', scatter_dimension=0, tiled=True)]
    dot_general x144 -> x24, matrix products: 176 us -> 44.2 us  [mm(): lax.dot_general(left, right, (dims, ((), ())), preferred_element_type=f32)]
    another operation x10 -> x0, loops' own time: 116 us -> none  [the longest x2 42.4 us: carried_in(): return lax.fori_loop(0, length, lap, start)]
    ppermute x2 -> x52, waiting for transfers between devices: 3.62 us -> 117 us  [the longest x40 81.2 us: swap(): return lax.ppermute(block, axis, [(0, 1), (1, 0)])]
    reduce_sum x40 -> x4, other arithmetic: 89.9 us -> 0.77 us  [norm_back(): jnp.mean(grad_unit * unit_values, axis=-1, keepdims=True)]
  transfers between devices with their start and end apart: 30 -> 60, of which waited for: 24 -> 49; matrix products, arithmetic and copies ran while one was open for 11% -> 11% of each run, Pallas kernels for 0% -> 5%
where the time goes in v1:
time: 797 us; the launch traced here: 792 us
  waiting for transfers between devices  533 us (67%)
  other arithmetic  60 us (8%)
  local copies, waits for them, and re-layouts  49 us (6%)
  Pallas kernels  47.6 us (6%)
  matrix products  44.2 us (6%)
  starting transfers between devices  42.6 us (5%)
  between operations  16.2 us (2%)
    reduce_scatter x2, waiting for transfers between devices, layer_backward(): lax.psum_scatter(feed_grad, 'dp', scatter_dimension=0, tiled=True)  181 us
    reduce_scatter x2, waiting for transfers between devices, layer_backward(): lax.psum_scatter(attn_grad, 'dp', scatter_dimension=0, tiled=True)  99.1 us
    all_gather x2, waiting for transfers between devices, shards(): attn.append(lax.all_gather(attn_parts[layer], 'dp', axis=0, tiled=True))  94.8 us
    ppermute x40, waiting for transfers between devices, swap(): return lax.ppermute(block, axis, [(0, 1), (1, 0)])  81.2 us
    pallas_call x12, Pallas kernels, call(): pl.pallas_call(body, out_shape=[jax.ShapeDtypeStruct(shape, kind) for sha...  47.6 us
    dot_general x24, matrix products, mm(): lax.dot_general(left, right, (dims, ((), ())), preferred_element_type=f32)  44.2 us
    all_gather x2, waiting for transfers between devices, shards(): feed.append(lax.all_gather(feed_parts[layer], 'dp', axis=0, tiled=True))  39.3 us
    ppermute x12, waiting for transfers between devices, scan_states(): other = lax.ppermute(pack, 'dp', [(i, i ^ step) for i in range(count)])  36.2 us
  transfers between devices with their start and end apart: 60, of which 49 were waited for; matrix products, arithmetic and copies ran while one was open for 11% of the time, Pallas kernels for 5%

profile of v1, /device:TPU:0, one launch (start us, length us, event | category | flops | bytes accessed | tf_op | source)
XLA Modules:
  0.0 792.2 jit_solution(8285684954166842574)
XLA Ops:
  30.3 45.7 %all-gather.5.cloned.1.call-done = bf16[1024,1152]{1,0:T(8,128)(2,1)} async-done(((bf16[128,1152]{1,0:T(8,128)(2,1)}), bf16[1024,1152]{1,0:T(8,128)(2,1)}) %all-gather.5.cloned.1.call-update) | async-done | bytes 2359312 | tf_op jit(solution)/shard_map/all_gather | solution.py:477
  80.2 49.1 %all-gather.9.cloned.1.call-done = bf16[1024,1152]{1,0:T(8,128)(2,1)} async-done(((bf16[128,1152]{1,0:T(8,128)(2,1)}), bf16[1024,1152]{1,0:T(8,128)(2,1)}) %all-gather.9.cloned.1.call-update) | async-done | bytes 2359312 | tf_op jit(solution)/shard_map/all_gather | solution.py:477
  136.8 4.1 shard_map.288
  142.1 5.5 collective-permute-done.4
  150.8 7.6 collective-permute-done.5
  160.5 4.1 shard_map.289
  173.9 6.7 collective-permute-done.8
  182.6 3.3 collective-permute-done.9
  187.9 21.5 %all-gather.7.cloned.1.call-done = bf16[1024,2112]{1,0:T(8,128)(2,1)} async-done(((bf16[128,2112]{1,0:T(8,128)(2,1)}), bf16[1024,2112]{1,0:T(8,128)(2,1)}) %all-gather.7.cloned.1.call-update) | async-done | bytes 4325392 | tf_op jit(solution)/shard_map/all_gather | solution.py:478
  220.3 6.1 collective-permute-done.13
  235.3 4.0 shard_map.291
  240.6 3.5 collective-permute-done.16
  247.4 7.9 collective-permute-done.17
  257.4 4.1 shard_map.292
  271.4 7.1 collective-permute-done.20
  285.6 17.8 %all-gather.11.cloned.1.call-done = bf16[1024,2112]{1,0:T(8,128)(2,1)} async-done(((bf16[128,2112]{1,0:T(8,128)(2,1)}), bf16[1024,2112]{1,0:T(8,128)(2,1)}) %all-gather.11.cloned.1.call-update) | async-done | bytes 4325392 | tf_op jit(solution)/shard_map/all_gather | solution.py:478
  313.6 4.1 collective-permute-done.29
  320.2 3.5 collective-permute-done.30
  331.7 3.2 collective-permute-done.32
  344.8 6.2 shard_map.295
  352.6 4.1 shard_map.296
  364.4 4.2 collective-permute-done.36
  368.9 4.8 collective-permute-done.24
  376.2 3.5 collective-permute-done.37
  387.5 4.0 collective-permute-done.40
  394.1 3.5 collective-permute-done.41
  418.5 6.4 shard_map.298
  425.6 4.1 shard_map.299
  487.6 26.8 %reduce-scatter.5.cloned.1.call-done = bf16[128,1152]{1,0:T(8,128)(2,1)} async-done(((bf16[1024,1152]{1,0:T(8,128)(2,1)}), bf16[128,1152]{1,0:T(8,128)(2,1)}) %reduce-scatter.5.cloned.1.call-update) | async-done | bytes 294928 | tf_op jit(solution)/shard_map/reduce_scatter | solution.py:400
  514.4 72.2 %reduce-scatter.7.cloned.1.call-done = bf16[128,1152]{1,0:T(8,128)(2,1)} async-done(((bf16[1024,1152]{1,0:T(8,128)(2,1)}), bf16[128,1152]{1,0:T(8,128)(2,1)}) %reduce-scatter.7.cloned.1.call-update) | async-done | bytes 294928 | tf_op jit(solution)/shard_map/reduce_scatter | solution.py:400
  595.5 86.0 %reduce-scatter.11.cloned.1.call-done = bf16[128,2112]{1,0:T(8,128)(2,1)} async-done(((bf16[1024,2112]{1,0:T(8,128)(2,1)}), bf16[128,2112]{1,0:T(8,128)(2,1)}) %reduce-scatter.11.cloned.1.call-update) | async-done | bytes 540688 | tf_op jit(solution)/shard_map/reduce_scatter | solution.py:356
  681.6 95.3 %reduce-scatter.9.cloned.1.call-done = bf16[128,2112]{1,0:T(8,128)(2,1)} async-done(((bf16[1024,2112]{1,0:T(8,128)(2,1)}), bf16[128,2112]{1,0:T(8,128)(2,1)}) %reduce-scatter.9.cloned.1.call-update) | async-done | bytes 540688 | tf_op jit(solution)/shard_map/reduce_scatter | solution.py:356
  (538 shorter events, 245.9 us)
Async XLA Ops:
  7.2 68.9 %all-gather.5.cloned.1.call-start = ((), (), s32[]{:S(2)}) async-start(), calls=%async_computation.4 | async-start | bytes 2654208 | tf_op jit(solution)/shard_map/all_gather | solution.py:477
  11.1 8.8 %collective-permute-start = (f32[64,28]{0,1:T(8,128)S(1)}, f32[64,28]{0,1:T(8,128)S(1)}, u32[]{:S(2)}, u32[]{:S(2)}) collective-permute-start(f32[64,28]{0,1:T(8,128)S(1)} %concatenate.193), channel_id=1, source_target_pairs={{0,1},{1,0},{2,3},{3,2},{4,5},{5,4},{6,7},{7,6},{8,9},{9,8},{10,11... | collective-permute-start | bytes 21512 | tf_op jit(solution)/shard_map/ppermute | solution.py:26
  23.8 105.4 %all-gather.9.cloned.1.call-start = ((), (), s32[]{:S(2)}) async-start(), calls=%async_computation.6 | async-start | bytes 2654208 | tf_op jit(solution)/shard_map/all_gather | solution.py:477
  24.6 184.8 %all-gather.7.cloned.1.call-start = ((), (), s32[]{:S(2)}) async-start(), calls=%async_computation.5 | async-start | bytes 5013504 | tf_op jit(solution)/shard_map/all_gather | solution.py:478
  29.8 273.7 %all-gather.11.cloned.1.call-start = ((), (), s32[]{:S(2)}) async-start(), calls=%async_computation.7 | async-start | bytes 5013504 | tf_op jit(solution)/shard_map/all_gather | solution.py:478
  78.6 52.6 %collective-permute-start.2 = (bf16[64,1024]{1,0:T(8,128)(2,1)S(1)}, bf16[64,1024]{1,0:T(8,128)(2,1)S(1)}, u32[]{:S(2)}, u32[]{:S(2)}) collective-permute-start(bf16[64,1024]{1,0:T(8,128)(2,1)S(1)} %multiply_convert_fusion.9), channel_id=1, source_target_pairs={{0,1},{1,0},{2,3},{3,2},{4,5},{5,4},{6,7},{7,6},{8,9},{9,8},{10,11... | collective-permute-start | bytes 393224 | tf_op jit(solution)/shard_map/ppermute | solution.py:26
  140.9 6.6 collective-permute-start.4
  149.2 9.2 %collective-permute-start.5 = (bf16[272,128]{1,0:T(8,128)(2,1)S(1)}, bf16[272,128]{1,0:T(8,128)(2,1)S(1)}, u32[]{:S(2)}, u32[]{:S(2)}) collective-permute-start(bf16[272,128]{1,0:T(8,128)(2,1)S(1)} %pad_maximum_fusion.24), channel_id=1, source_target_pairs={{0,4},{2,6},{4,0},{6,2},{8,12},{10,14},{12,8},{14,10},{1,5},{3,7},... | collective-permute-start | bytes 208904 | tf_op jit(solution)/shard_map/ppermute | solution.py:245
  159.4 6.0 collective-permute-start.6
  172.3 8.4 %collective-permute-start.8 = (f32[64,1024]{1,0:T(8,128)S(1)}, f32[64,1024]{1,0:T(8,128)S(1)}, u32[]{:S(2)}, u32[]{:S(2)}) collective-permute-start(f32[64,1024]{1,0:T(8,128)S(1)} %select_bitcast_fusion.25), channel_id=1, source_target_pairs={{0,1},{1,0},{2,3},{3,2},{4,5},{5,4},{6,7},{7,6},{8,9},{9,8},{10,11... | collective-permute-start | bytes 786440 | tf_op jit(solution)/shard_map/ppermute | solution.py:26
  180.9 5.0 collective-permute-start.9
  218.0 8.4 %collective-permute-start.13 = (f32[64,1024]{1,0:T(8,128)S(1)}, f32[64,1024]{1,0:T(8,128)S(1)}, u32[]{:S(2)}, u32[]{:S(2)}) collective-permute-start(f32[64,1024]{1,0:T(8,128)S(1)} %select_bitcast_fusion.22), channel_id=1, source_target_pairs={{0,1},{1,0},{2,3},{3,2},{4,5},{5,4},{6,7},{7,6},{8,9},{9,8},{10,11... | collective-permute-start | bytes 786440 | tf_op jit(solution)/shard_map/ppermute | solution.py:26
  226.6 5.0 collective-permute-start.14
  228.2 286.2 %reduce-scatter.5.cloned.1.call-start = ((), (), s32[]{:S(2)}) async-start(), calls=%async_computation.8 | async-start | bytes 2654208 | tf_op jit(solution)/shard_map/reduce_scatter | solution.py:400
  245.7 9.5 %collective-permute-start.17 = (bf16[272,128]{1,0:T(8,128)(2,1)S(1)}, bf16[272,128]{1,0:T(8,128)(2,1)S(1)}, u32[]{:S(2)}, u32[]{:S(2)}) collective-permute-start(bf16[272,128]{1,0:T(8,128)(2,1)S(1)} %pad_maximum_fusion.26), channel_id=1, source_target_pairs={{0,4},{2,6},{4,0},{6,2},{8,12},{10,14},{12,8},{14,10},{1,5},{3,7},... | collective-permute-start | bytes 208904 | tf_op jit(solution)/shard_map/ppermute | solution.py:245
  256.2 6.0 collective-permute-start.18
  269.2 9.2 %collective-permute-start.20 = (f32[64,1024]{1,0:T(8,128)S(1)}, f32[64,1024]{1,0:T(8,128)S(1)}, u32[]{:S(2)}, u32[]{:S(2)}) collective-permute-start(f32[64,1024]{1,0:T(8,128)S(1)} %select_bitcast_fusion.19), channel_id=1, source_target_pairs={{0,1},{1,0},{2,3},{3,2},{4,5},{5,4},{6,7},{7,6},{8,9},{9,8},{10,11... | collective-permute-start | bytes 786440 | tf_op jit(solution)/shard_map/ppermute | solution.py:26
  271.0 9.9 %collective-permute-start.26 = (bf16[64,1024]{1,0:T(8,128)(2,1)S(1)}, bf16[64,1024]{1,0:T(8,128)(2,1)S(1)}, u32[]{:S(2)}, u32[]{:S(2)}) collective-permute-start(bf16[64,1024]{1,0:T(8,128)(2,1)S(1)} %dynamic-slice_convert_fusion), channel_id=1, source_target_pairs={{0,1},{1,0},{2,3},{3,2},{4,5},{5,4},{6,7},{7,6},{8,9},{9,8},{10,11... | collective-permute-start | bytes 393224 | tf_op jit(solution)/shard_map/ppermute | solution.py:26
  278.7 5.0 collective-permute-start.21
  312.1 5.6 collective-permute-start.29
  342.2 8.8 %collective-permute-start.34 = (bf16[272,128]{1,0:T(8,128)(2,1)}, bf16[272,128]{1,0:T(8,128)(2,1)}, u32[]{:S(2)}, u32[]{:S(2)}) collective-permute-start(bf16[272,128]{1,0:T(8,128)(2,1)} %pad_maximum_fusion.29), channel_id=1, source_target_pairs={{0,8},{2,10},{4,12},{6,14},{8,0},{10,2},{12,4},{14,6},{1,9},{3,11}... | collective-permute-start | bytes 208904 | tf_op jit(solution)/shard_map/ppermute | solution.py:245
  344.8 15.7 %collective-permute-start.23 = (f32[2,64,1024]{2,1,0:T(8,128)}, f32[2,64,1024]{2,1,0:T(8,128)}, u32[]{:S(2)}, u32[]{:S(2)}) collective-permute-start(f32[2,64,1024]{2,1,0:T(8,128)} %select_bitcast_fusion.4), channel_id=1, source_target_pairs={{0,16},{16,0},{1,17},{17,1},{2,18},{18,2},{3,19},{19,3},{4,20},{20... | collective-permute-start | bytes 1572872 | tf_op jit(solution)/shard_map/ppermute | solution.py:26
  362.2 6.4 collective-permute-start.36
  363.8 9.9 %collective-permute-start.24 = (f32[64,1024]{1,0:T(8,128)S(1)}, f32[64,1024]{1,0:T(8,128)S(1)}, u32[]{:S(2)}, u32[]{:S(2)}) collective-permute-start(f32[64,1024]{1,0:T(8,128)S(1)} %select_bitcast_fusion.16), channel_id=1, source_target_pairs={{0,1},{1,0},{2,3},{3,2},{4,5},{5,4},{6,7},{7,6},{8,9},{9,8},{10,11... | collective-permute-start | bytes 786440 | tf_op jit(solution)/shard_map/ppermute | solution.py:26
  386.0 5.6 collective-permute-start.40
  415.6 9.3 %collective-permute-start.45 = (bf16[272,128]{1,0:T(8,128)(2,1)S(1)}, bf16[272,128]{1,0:T(8,128)(2,1)S(1)}, u32[]{:S(2)}, u32[]{:S(2)}) collective-permute-start(bf16[272,128]{1,0:T(8,128)(2,1)S(1)} %pad_maximum_fusion.31), channel_id=1, source_target_pairs={{0,8},{2,10},{4,12},{6,14},{8,0},{10,2},{12,4},{14,6},{1,9},{3,11}... | collective-permute-start | bytes 208904 | tf_op jit(solution)/shard_map/ppermute | solution.py:245
  446.2 140.5 %reduce-scatter.7.cloned.1.call-start = ((), (), s32[]{:S(2)}) async-start(), calls=%async_computation.9 | async-start | bytes 2654208 | tf_op jit(solution)/shard_map/reduce_scatter | solution.py:400
  459.8 221.8 %reduce-scatter.11.cloned.1.call-start = ((), (), s32[]{:S(2)}) async-start(), calls=%async_computation.11 | async-start | bytes 5013504 | tf_op jit(solution)/shard_map/reduce_scatter | solution.py:356
  468.9 307.9 %reduce-scatter.9.cloned.1.call-start = ((), (), s32[]{:S(2)}) async-start(), calls=%async_computation.10 | async-start | bytes 5013504 | tf_op jit(solution)/shard_map/reduce_scatter | solution.py:356
  481.5 5.6 collective-permute-start.47
  487.5 100.3 %collective-permute-start.48 = (f32[64,1024]{1,0:T(8,128)S(1)}, f32[64,1024]{1,0:T(8,128)S(1)}, u32[]{:S(2)}, u32[]{:S(2)}) collective-permute-start(f32[64,1024]{1,0:T(8,128)S(1)} %get-tuple-element.209), channel_id=1, source_target_pairs={{0,16},{16,0},{1,17},{17,1},{2,18},{18,2},{3,19},{19,3},{4,20},{20... | collective-permute-start | bytes 786440 | tf_op jit(solution)/shard_map/ppermute | solution.py:26
  589.4 5.2 collective-permute-start.50
  (97 other events, 665.7 us)
Sparse Core Ops, SparseCore 0:
  23.9 52.0 all-gather.4
  78.8 50.3 all-gather.8
  132.0 77.3 all-gather.6
  228.3 75.0 all-gather.10
  446.3 68.0 reduce-scatter.4
  517.8 68.8 reduce-scatter.6
  590.3 91.2 reduce-scatter.10
  685.2 91.6 reduce-scatter.8
